TPU v7x, 32 devices: a whole 2x2x4 slice. The times are simulated.
32 devices in a mesh: dp: 8 (over y, x, core), mp: 4 (over z).
Axes of the slice: x: 2, y: 2, z: 4, core: 2. Of those that a mesh axis runs over, the one named last changes fastest.
Arguments:
- tokens: bfloat16 [320, 4096], P('dp'), may hold values from -6 to 6
- attn_gain: float32 [4096], replicated, may hold values from 0.1 to 1.9
- head_gain: float32 [4096], replicated, may hold values from 0.1 to 1.9
- qkv_weight: bfloat16 [4096, 3, 4096], P('dp', None, 'mp'), may hold values from -0.09375 to 0.09375
- out_weight: bfloat16 [4096, 4096], P('mp', 'dp'), may hold values from -0.09375 to 0.09375
- head_weight: bfloat16 [4096, 1024], P('mp'), may hold values from -0.09375 to 0.09375
- key_cache: bfloat16 [320, 64, 4096], P('dp', None, 'mp'), may hold values from -400 to 400
- value_cache: bfloat16 [320, 64, 4096], P('dp', None, 'mp'), may hold values from -6 to 6
- parents: int32 [320], P('dp'), may hold values from 0 to 19
- allowed: int32 [320, 2], P('dp'), may hold values from 0 to 7, all different within a row
Outputs:
- new_stream: bfloat16 [320, 4096], P('dp')
- next_logits: float32 [320, 256], P('dp', 'mp')
Inputs may be any that keep to these rules, and one draw needn't show every extreme that they name: `parents`: a beam's parent is a beam of the same query. `allowed`: the 2 block ids of a beam differ.
All inputs are finite; a program needn't handle non-finite values.
Results may differ from a plain program's by a relative error of at most 0.017.
Values may be sent and summed in bfloat16 or wider, within the bound.
No kernel may reach another device: no remote copies, remote signals or barrier semaphores. Data moves between devices by JAX's collectives and lax.ppermute only.
A program may use at most 128 MiB of HBM per device.

v0:
```python
import jax
import jax.numpy as jnp
from jax import lax
from jax.sharding import PartitionSpec as P

HEAD = 128
BEAMS = 20
BLOCK = 128


def root_norm(values, gain_vec):
    float_values = values.astype(jnp.float32)
    factor = lax.rsqrt(jnp.mean(float_values * float_values, axis=-1, keepdims=True) + 1e-06)
    return float_values * factor * gain_vec


def select_blocks(whole_logits, allowed):
    block_count = whole_logits.shape[1] // BLOCK
    block_list = whole_logits.reshape(whole_logits.shape[0], block_count, BLOCK)
    one_hot_rows = (
        allowed[:, :, None] == jnp.arange(block_count, dtype=jnp.int32)[None, None, :]
    ).astype(jnp.float32)
    selected_token = jnp.einsum(
        "ioh,ihp->iop", one_hot_rows, block_list, precision=lax.Precision.HIGHEST
    )
    return selected_token.reshape(whole_logits.shape[0], -1)


def on_device(
    tokens,
    attn_gain,
    head_gain,
    qkv_weight,
    out_weight,
    head_weight,
    key_cache,
    value_cache,
    parents,
    allowed,
):
    row_count = tokens.shape[0]
    normed = root_norm(tokens, attn_gain).astype(jnp.bfloat16)
    spread = lax.all_to_all(normed, "dp", split_axis=1, concat_axis=0, tiled=True)
    depth_part = qkv_weight.shape[0]
    head_width = qkv_weight.shape[2]
    flat_qkv = qkv_weight.reshape(depth_part, 3 * head_width)
    projected = lax.psum_scatter(
        jnp.dot(spread, flat_qkv, preferred_element_type=jnp.float32),
        "dp",
        scatter_dimension=0,
        tiled=True,
    )
    projected = projected.astype(jnp.bfloat16).reshape(row_count, 3, head_width)
    local_heads = head_width // HEAD
    length = key_cache.shape[1] + 1
    source = jnp.arange(row_count, dtype=jnp.int32) // BEAMS * BEAMS + parents
    key_rows = jnp.concatenate(
        [jnp.take(key_cache, source, axis=0), projected[:, 1][:, None]], axis=1
    )
    value_rows = jnp.concatenate(
        [jnp.take(value_cache, source, axis=0), projected[:, 2][:, None]], axis=1
    )
    key_rows = key_rows.reshape(row_count, length, local_heads, HEAD)
    value_rows = value_rows.reshape(row_count, length, local_heads, HEAD)
    queries = projected[:, 0].reshape(row_count, local_heads, HEAD)
    scores = jnp.einsum(
        "thd,tjhd->thj", queries, key_rows, preferred_element_type=jnp.float32
    ) * HEAD ** (-0.5)
    softmax_w = jax.nn.softmax(scores, axis=-1).astype(jnp.bfloat16)
    attention_result = jnp.einsum(
        "thj,tjhd->thd", softmax_w, value_rows, preferred_element_type=jnp.float32
    )
    attention_result = attention_result.astype(jnp.bfloat16).reshape(row_count, head_width)
    partial_value = jnp.dot(
        attention_result,
        lax.all_gather(out_weight, "dp", axis=1, tiled=True),
        preferred_element_type=jnp.float32,
    )
    attn_out = lax.psum(partial_value, "mp")
    stream = tokens.astype(jnp.float32) + attn_out
    head_input = root_norm(stream, head_gain).astype(jnp.bfloat16)
    depth_rows = head_weight.shape[0]
    own_part = lax.dynamic_slice_in_dim(
        head_input, lax.axis_index("mp") * depth_rows, depth_rows, 1
    )
    partial_logits = jnp.dot(own_part, head_weight, preferred_element_type=jnp.float32)
    next_logits = lax.psum_scatter(
        select_blocks(partial_logits, allowed).astype(jnp.bfloat16),
        "mp",
        scatter_dimension=1,
        tiled=True,
    ).astype(jnp.float32)
    return (stream.astype(jnp.bfloat16), next_logits)


def solution(mesh):
    in_specs = (
        P("dp", None),
        P(),
        P(),
        P("dp", None, "mp"),
        P("mp", "dp"),
        P("mp", None),
        P("dp", None, "mp"),
        P("dp", None, "mp"),
        P("dp"),
        P("dp", None),
    )
    out_specs = (P("dp", None), P("dp", "mp"))
    return jax.shard_map(
        on_device, mesh=mesh, in_specs=in_specs, out_specs=out_specs, check_vma=False
    )
```

profile of v0, /device:TPU:0, one launch (start us, length us, event | category | flops | bytes accessed | tf_op | source)
XLA Modules:
  0.0 211.9 jit_solution(16103499963755374255)
XLA Ops:
  7.2 0.0 copy-start
  7.2 1.3 fusion.11
  8.5 1.1 fusion.13
  9.6 0.7 copy.55
  10.4 5.2 %all-to-all-start = ((bf16[40,8,512]{2,0,1:T(8,128)(2,1)}), bf16[40,8,512]{2,0,1:T(8,128)(2,1)S(1)}, u32[]{:S(2)}, u32[]{:S(2)}) async-start(bf16[40,8,512]{2,0,1:T(8,128)(2,1)} %bitcast.32), calls=%async_computation | async-start | bytes 655360 | tf_op jit(solution)/shard_map/all_to_all | solution.py:43
  15.6 0.0 reduce-scatter.5.cloned.1.call-start
  15.6 4.7 %copy.24 = bf16[512,3,1024]{0,2,1:T(8,128)(2,1)} copy(bf16[512,3,1024]{2,0,1:T(8,128)(2,1)} %param.15) | data formatting | bytes 6291456 | tf_op args[3]
  20.3 2.9 %all-to-all-done = bf16[40,8,512]{2,0,1:T(8,128)(2,1)S(1)} async-done(((bf16[40,8,512]{2,0,1:T(8,128)(2,1)}), bf16[40,8,512]{2,0,1:T(8,128)(2,1)S(1)}, u32[]{:S(2)}, u32[]{:S(2)}) %all-to-all-start) | async-done | bytes 327712 | tf_op jit(solution)/shard_map/all_to_all | solution.py:43
  23.2 0.0 copy-start.3
  23.2 5.0 %fusion.35 = f32[320,3072]{1,0:T(8,128)} fusion(bf16[320,512]{1,0:T(8,128)(2,1)S(1)} %bitcast.34, bf16[512,3072]{0,1:T(8,128)(2,1)} %bitcast.33), kind=kOutput, calls=%fused_computation.57 | convolution fusion | flops 1006632960 | bytes 7405568 | tf_op jit(solution)/shard_map/dot_general | solution.py:48
  28.2 0.0 reduce-scatter.5.cloned.1.call-update
  28.2 0.0 all-gather.2.cloned.1.call-start
  28.3 0.7 all-gather.2.cloned.1.call-update
  29.0 0.0 all-reduce.2.cloned.1.call-start
  29.0 0.0 copy-done.3
  29.1 7.2 %gather_fusion = bf16[40,64,1024]{2,1,0:T(8,128)(2,1)} fusion(bf16[40,64,1024]{2,1,0:T(8,128)(2,1)} %param.18, s32[1024]{0:T(1024)S(1)} %pad_clamp_fusion), kind=kCustom, calls=%fused_computation.clone | custom fusion | bytes 10485920 | tf_op jit(solution)/shard_map/jit(_take)/gather | solution.py:58
  36.3 7.6 %gather_fusion.1 = bf16[40,64,1024]{2,1,0:T(8,128)(2,1)} fusion(bf16[40,64,1024]{2,1,0:T(8,128)(2,1)} %param.19, s32[1024]{0:T(1024)S(1)} %pad_clamp_fusion), kind=kCustom, calls=%fused_computation.1.clone | custom fusion | bytes 10485920 | tf_op jit(solution)/shard_map/jit(_take)/gather | solution.py:61
  43.9 9.1 %broadcast_select_fusion.1 = (bf16[40,64,1024]{2,1,0:T(8,128)(2,1)}, bf16[40,64,1024]{2,1,0:T(8,128)(2,1)}) fusion(bf16[40,64,1024]{2,1,0:T(8,128)(2,1)} %gather_fusion, pred[40]{0:T(512)(128)(4,1)S(1)} %get-tuple-element.5, bf16[40,64,1024]{2,1,0:T(8,128)(2,1)} %gather_fusion.1), kind=kLoop, calls=%fused_computation.11 | loop fusion | flops 5242880 | bytes 20971560 | tf_op jit(solution)/shard_map/jit(_take)/select_n | solution.py:58
  52.9 24.6 %reduce-scatter.5.cloned.1.call-done = f32[40,3072]{1,0:T(8,128)} async-done(((f32[320,3072]{1,0:T(8,128)}), f32[40,3072]{1,0:T(8,128)}) %reduce-scatter.5.cloned.1.call-update) | async-done | bytes 491536 | tf_op jit(solution)/shard_map/reduce_scatter | solution.py:47
  77.6 1.1 convert_element_type.34
  78.6 0.4 reshape.54
  79.0 0.3 fusion.32
  79.3 11.1 %pad_maximum_fusion = (bf16[40,65,1024]{2,1,0:T(8,128)(2,1)}, bf16[40,65,1024]{2,1,0:T(8,128)(2,1)}) fusion(bf16[40,1,1024]{2,1,0:T(2,128)(2,1)S(1)} %get-tuple-element.7, bf16[40,64,1024]{2,1,0:T(8,128)(2,1)} %get-tuple-element.9, bf16[40,1,1024]{2,1,0:T(2,128)(2,1)S(1)} %get-tuple-element.8, bf16[40,64,1024]{2,1,0:T(8,128)(2,1)} %get-tuple-element.10), kind=kLoop, calls=%fused_computation.4 | loop fusion | flops 21299200 | bytes 21299200 | tf_op jit(solution)/shard_map/concatenate | solution.py:57
  90.4 9.1 %reshape.86 = bf16[40,65,8,128]{3,2,1,0:T(8,128)(2,1)} reshape(bf16[40,65,1024]{2,1,0:T(8,128)(2,1)} %get-tuple-element.11) | data formatting | bytes 10649600 | tf_op jit(solution)/shard_map/reshape | solution.py:63
  99.5 9.3 %reshape.87 = bf16[40,65,8,128]{3,2,1,0:T(8,128)(2,1)} reshape(bf16[40,65,1024]{2,1,0:T(8,128)(2,1)} %get-tuple-element.12) | data formatting | bytes 10649600 | tf_op jit(solution)/shard_map/reshape | solution.py:64
  108.8 5.9 %fusion.4 = f32[40,8,1,65]{3,2,1,0:T(1,128)S(1)} fusion(bf16[40,65,8,128]{3,2,1,0:T(8,128)(2,1)} %reshape.86, bf16[40,3,1024]{2,1,0:T(4,128)(2,1)S(1)} %reshape.54), kind=kOutput, calls=%fused_computation.8 | convolution fusion | flops 5324800 | bytes 5571840 | tf_op jit(solution)/shard_map/thd,tjhd->thj/dot_general | solution.py:66
  114.6 0.2 fusion.10
  114.9 4.2 %fusion.2 = f32[40,8,1,128]{3,2,1,0:T(1,128)S(1)} fusion(bf16[40,65,8,128]{3,2,1,0:T(8,128)(2,1)} %reshape.87, bf16[40,8,65,1]{2,1,0,3:T(8,128)(2,1)S(1)} %fusion.10), kind=kOutput, calls=%fused_computation.6 | convolution fusion | flops 5324800 | bytes 5530240 | tf_op jit(solution)/shard_map/thj,tjhd->thd/dot_general | solution.py:70
  119.1 16.2 %all-gather.2.cloned.1.call-done = bf16[1024,4096]{1,0:T(8,128)(2,1)} async-done(((bf16[1024,512]{1,0:T(8,128)(2,1)}), bf16[1024,4096]{1,0:T(8,128)(2,1)}) %all-gather.2.cloned.1.call-update) | async-done | bytes 8388624 | tf_op jit(solution)/shard_map/all_gather | solution.py:76
  135.3 0.0 copy-start.2
  135.3 0.0 copy-start.1
  135.3 5.9 %fusion.19 = f32[40,4096]{1,0:T(8,128)} fusion(bf16[1024,4096]{1,0:T(8,128)(2,1)} %all-gather.2.cloned.1.call-done, bf16[5,8,8,128]{3,2,1,0:T(8,128)(2,1)S(1)} %bitcast.36), kind=kOutput, calls=%fused_computation.34 | convolution fusion | flops 335544320 | bytes 9125888 | tf_op jit(solution)/shard_map/dot_general | solution.py:74
  141.2 0.0 all-reduce.2.cloned.1.call-update
  141.2 0.0 reduce-scatter.7.cloned.1.call-start
  141.3 0.0 copy-done.2
  141.3 0.1 copy.27
  141.4 0.7 dynamic-slice
  142.1 39.9 %all-reduce.2.cloned.1.call-done = f32[40,4096]{1,0:T(8,128)} async-done(((f32[40,4096]{1,0:T(8,128)}), f32[40,4096]{1,0:T(8,128)}) %all-reduce.2.cloned.1.call-update) | async-done | bytes 655376 | tf_op jit(solution)/shard_map/psum | solution.py:79
  181.9 0.0 copy-done.1
  181.9 1.3 multiply_reduce_fusion
  183.2 0.0 copy-done
  183.2 0.5 convolution_bitcast_fusion
  183.8 0.3 convolution_convert_fusion
  184.1 0.7 copy.40
  184.9 0.0 reduce-scatter.7.cloned.1.call-update
  184.9 0.8 convert_element_type.37
  185.7 18.2 %reduce-scatter.7.cloned.1.call-done = bf16[64,40]{1,0:T(8,128)(2,1)} async-done(((bf16[256,40]{1,0:T(8,128)(2,1)}), bf16[64,40]{1,0:T(8,128)(2,1)}) %reduce-scatter.7.cloned.1.call-update) | async-done | bytes 5136
  203.9 0.8 copy.39
  204.7 0.6 convert_element_type.41
  (6 shorter events, 0.1 us)
Async XLA Ops:
  7.2 176.1 %copy-start = (bf16[1024,1024]{1,0:T(8,128)(2,1)S(1)}, bf16[1024,1024]{1,0:T(8,128)(2,1)}, u32[]{:S(2)}) copy-start(bf16[1024,1024]{1,0:T(8,128)(2,1)} %param.17) | copy-start | bytes 6291460
  10.4 12.8 %all-to-all-start = ((bf16[40,8,512]{2,0,1:T(8,128)(2,1)}), bf16[40,8,512]{2,0,1:T(8,128)(2,1)S(1)}, u32[]{:S(2)}, u32[]{:S(2)}) async-start(bf16[40,8,512]{2,0,1:T(8,128)(2,1)} %bitcast.32), calls=%async_computation | async-start | bytes 655360 | tf_op jit(solution)/shard_map/all_to_all | solution.py:43
  15.6 62.0 %reduce-scatter.5.cloned.1.call-start = ((), (), s32[]{:S(2)}) async-start(), calls=%async_computation.3 | async-start | bytes 4423680 | tf_op jit(solution)/shard_map/reduce_scatter | solution.py:47
  23.2 5.8 %copy-start.3 = (s32[40]{0:T(128)S(1)}, s32[40]{0:T(128)}, u32[]{:S(2)}) copy-start(s32[40]{0:T(128)} %param.20) | copy-start | bytes 484
  28.2 107.1 %all-gather.2.cloned.1.call-start = ((), (), s32[]{:S(2)}) async-start(), calls=%async_computation.4 | async-start | bytes 9437184 | tf_op jit(solution)/shard_map/all_gather | solution.py:76
  29.0 153.0 %all-reduce.2.cloned.1.call-start = ((), (), s32[]{:S(2)}) async-start(), calls=%async_computation.5 | async-start | bytes 1310720 | tf_op jit(solution)/shard_map/psum | solution.py:79
  135.3 6.0 %copy-start.2 = (s32[40,2]{0,1:T(2,128)S(1)}, s32[40,2]{0,1:T(2,128)}, u32[]{:S(2)}) copy-start(s32[40,2]{0,1:T(2,128)} %param.21) | copy-start | bytes 964
  135.3 46.6 %copy-start.1 = (bf16[40,4096]{1,0:T(8,128)(2,1)S(1)}, bf16[40,4096]{1,0:T(8,128)(2,1)}, u32[]{:S(2)}) copy-start(bf16[40,4096]{1,0:T(8,128)(2,1)} %param.12) | copy-start | bytes 983044
  141.2 62.7 %reduce-scatter.7.cloned.1.call-start = ((), (), s32[]{:S(2)}) async-start(), calls=%async_computation.6 | async-start | bytes 81920
Sparse Core Ops, SparseCore 0:
  28.3 49.1 reduce-scatter.4
  79.4 55.8 all-gather.1
  141.4 40.5 all-reduce.1
  185.0 18.8 reduce-scatter.6
where the time goes:
time: 213 us; the launch traced here: 212 us
  waiting for transfers between devices  103 us (48%)
  local copies, waits for them, and re-layouts  41.6 us (20%)
  other arithmetic  26.6 us (12%)
  matrix products  21.8 us (10%)
  between operations  13.9 us (7%)
  starting transfers between devices  5.36 us (3%)
    psum x1, waiting for transfers between devices, on_device(): attn_out = lax.psum(partial_value, 'mp')  39.9 us
    reduce_scatter x1, waiting for transfers between devices, on_device(): lax.psum_scatter(jnp.dot(spread, flat_qkv, preferred_element_type=jnp.flo...  24.6 us
    unnamed x5, waiting for transfers between devices  19 us
    all_gather x1, waiting for transfers between devices, on_device(): lax.all_gather(out_weight, 'dp', axis=1, tiled=True)  16.2 us
    concatenate x1, other arithmetic, on_device(): jnp.concatenate([jnp.take(key_cache, source, axis=0), projected[:, 1][:,...  11.1 us
    reshape x1, local copies, waits for them, and re-layouts, on_device(): value_rows = value_rows.reshape(row_count, length, local_heads, HEAD)  9.25 us
    reshape x1, local copies, waits for them, and re-layouts, on_device(): key_rows = key_rows.reshape(row_count, length, local_heads, HEAD)  9.11 us
    select_n x1, other arithmetic, on_device(): jnp.take(key_cache, source, axis=0)  9.08 us
  transfers between devices with their start and end apart: 5, of which 5 were waited for; matrix products, arithmetic and copies ran while one was open for 34% of the time, Pallas kernels for 0%

commit v1 on v0

--- a/solution.py
+++ b/solution.py
@@ -76,7 +76,7 @@
         lax.all_gather(out_weight, "dp", axis=1, tiled=True),
         preferred_element_type=jnp.float32,
     )
-    attn_out = lax.psum(partial_value, "mp")
+    attn_out = jnp.sum(lax.all_gather(partial_value, "mp"), axis=0)
     stream = tokens.astype(jnp.float32) + attn_out
     head_input = root_norm(stream, head_gain).astype(jnp.bfloat16)
     depth_rows = head_weight.shape[0]

time: 213 us -> 229 us (1.075)
  waiting for transfers between devices: 103 us -> 116 us
  other arithmetic: 26.6 us -> 29.4 us
    all_gather x0 -> x1, waiting for transfers between devices: none -> 54.1 us  [on_device(): attn_out = jnp.sum(lax.all_gather(partial_value, 'mp'), axis=0)]
    psum x1 -> x0, waiting for transfers between devices: 39.9 us -> none  [on_device(): attn_out = lax.psum(partial_value, 'mp')]
    reduce_sum x0 -> x1, other arithmetic: none -> 2.81 us  [on_device(): attn_out = jnp.sum(lax.all_gather(partial_value, 'mp'), axis=0)]
  transfers between devices with their start and end apart: 5 -> 5, of which waited for: 5 -> 5; matrix products, arithmetic and copies ran while one was open for 34% -> 31% of each run, Pallas kernels for 0% -> 0%
where the time goes in v1:
time: 229 us; the launch traced here: 228 us
  waiting for transfers between devices  116 us (51%)
  local copies, waits for them, and re-layouts  41.6 us (18%)
  other arithmetic  29.4 us (13%)
  matrix products  21.8 us (10%)
  between operations  13.9 us (6%)
  starting transfers between devices  5.36 us (2%)
    all_gather x1, waiting for transfers between devices, on_device(): attn_out = jnp.sum(lax.all_gather(partial_value, 'mp'), axis=0)  54.1 us
    reduce_scatter x1, waiting for transfers between devices, on_device(): lax.psum_scatter(jnp.dot(spread, flat_qkv, preferred_element_type=jnp.flo...  24.6 us
    unnamed x5, waiting for transfers between devices  18.2 us
    all_gather x1, waiting for transfers between devices, on_device(): lax.all_gather(out_weight, 'dp', axis=1, tiled=True)  16.2 us
    concatenate x1, other arithmetic, on_device(): jnp.concatenate([jnp.take(key_cache, source, axis=0), projected[:, 1][:,...  11.1 us
    reshape x1, local copies, waits for them, and re-layouts, on_device(): value_rows = value_rows.reshape(row_count, length, local_heads, HEAD)  9.25 us
    reshape x1, local copies, waits for them, and re-layouts, on_device(): key_rows = key_rows.reshape(row_count, length, local_heads, HEAD)  9.11 us
    select_n x1, other arithmetic, on_device(): jnp.take(key_cache, source, axis=0)  9.08 us
  transfers between devices with their start and end apart: 5, of which 5 were waited for; matrix products, arithmetic and copies ran while one was open for 31% of the time, Pallas kernels for 0%

profile of v1, /device:TPU:0, one launch (start us, length us, event | category | flops | bytes accessed | tf_op | source)
XLA Modules:
  0.0 228.1 jit_solution(9385093844057027077)
XLA Ops:
  7.2 0.0 copy-start
  7.2 1.3 fusion.11
  8.5 1.1 fusion.13
  9.6 0.7 copy.59
  10.4 5.2 %all-to-all-start = ((bf16[40,8,512]{2,0,1:T(8,128)(2,1)}), bf16[40,8,512]{2,0,1:T(8,128)(2,1)S(1)}, u32[]{:S(2)}, u32[]{:S(2)}) async-start(bf16[40,8,512]{2,0,1:T(8,128)(2,1)} %bitcast.33), calls=%async_computation | async-start | bytes 655360 | tf_op jit(solution)/shard_map/all_to_all | solution.py:43
  15.6 0.0 reduce-scatter.5.cloned.1.call-start
  15.6 4.7 %copy.28 = bf16[512,3,1024]{0,2,1:T(8,128)(2,1)} copy(bf16[512,3,1024]{2,0,1:T(8,128)(2,1)} %param.15) | data formatting | bytes 6291456 | tf_op args[3]
  20.3 2.9 %all-to-all-done = bf16[40,8,512]{2,0,1:T(8,128)(2,1)S(1)} async-done(((bf16[40,8,512]{2,0,1:T(8,128)(2,1)}), bf16[40,8,512]{2,0,1:T(8,128)(2,1)S(1)}, u32[]{:S(2)}, u32[]{:S(2)}) %all-to-all-start) | async-done | bytes 327712 | tf_op jit(solution)/shard_map/all_to_all | solution.py:43
  23.2 0.0 copy-start.3
  23.2 5.0 %fusion.35 = f32[320,3072]{1,0:T(8,128)} fusion(bf16[320,512]{1,0:T(8,128)(2,1)S(1)} %bitcast.36, bf16[512,3072]{0,1:T(8,128)(2,1)} %bitcast.34), kind=kOutput, calls=%fused_computation.57 | convolution fusion | flops 1006632960 | bytes 7405568 | tf_op jit(solution)/shard_map/dot_general | solution.py:48
  28.2 0.0 reduce-scatter.5.cloned.1.call-update
  28.2 0.0 all-gather.4.cloned.1.call-start
  28.3 0.7 all-gather.4.cloned.1.call-update
  29.0 0.0 all-gather.6.cloned.1.call-start
  29.0 0.0 copy-done.3
  29.1 7.2 %gather_fusion = bf16[40,64,1024]{2,1,0:T(8,128)(2,1)} fusion(bf16[40,64,1024]{2,1,0:T(8,128)(2,1)} %param.18, s32[1024]{0:T(1024)S(1)} %pad_clamp_fusion), kind=kCustom, calls=%fused_computation.clone | custom fusion | bytes 10485920 | tf_op jit(solution)/shard_map/jit(_take)/gather | solution.py:58
  36.3 7.6 %gather_fusion.1 = bf16[40,64,1024]{2,1,0:T(8,128)(2,1)} fusion(bf16[40,64,1024]{2,1,0:T(8,128)(2,1)} %param.19, s32[1024]{0:T(1024)S(1)} %pad_clamp_fusion), kind=kCustom, calls=%fused_computation.1.clone | custom fusion | bytes 10485920 | tf_op jit(solution)/shard_map/jit(_take)/gather | solution.py:61
  43.9 9.1 %broadcast_select_fusion.1 = (bf16[40,64,1024]{2,1,0:T(8,128)(2,1)}, bf16[40,64,1024]{2,1,0:T(8,128)(2,1)}) fusion(bf16[40,64,1024]{2,1,0:T(8,128)(2,1)} %gather_fusion, pred[40]{0:T(512)(128)(4,1)S(1)} %get-tuple-element.5, bf16[40,64,1024]{2,1,0:T(8,128)(2,1)} %gather_fusion.1), kind=kLoop, calls=%fused_computation.11 | loop fusion | flops 5242880 | bytes 20971560 | tf_op jit(solution)/shard_map/jit(_take)/select_n | solution.py:58
  52.9 24.6 %reduce-scatter.5.cloned.1.call-done = f32[40,3072]{1,0:T(8,128)} async-done(((f32[320,3072]{1,0:T(8,128)}), f32[40,3072]{1,0:T(8,128)}) %reduce-scatter.5.cloned.1.call-update) | async-done | bytes 491536 | tf_op jit(solution)/shard_map/reduce_scatter | solution.py:47
  77.6 1.1 convert_element_type.34
  78.6 0.4 reshape.54
  79.0 0.3 fusion.32
  79.3 11.1 %pad_maximum_fusion = (bf16[40,65,1024]{2,1,0:T(8,128)(2,1)}, bf16[40,65,1024]{2,1,0:T(8,128)(2,1)}) fusion(bf16[40,1,1024]{2,1,0:T(2,128)(2,1)S(1)} %get-tuple-element.7, bf16[40,64,1024]{2,1,0:T(8,128)(2,1)} %get-tuple-element.9, bf16[40,1,1024]{2,1,0:T(2,128)(2,1)S(1)} %get-tuple-element.8, bf16[40,64,1024]{2,1,0:T(8,128)(2,1)} %get-tuple-element.10), kind=kLoop, calls=%fused_computation.4 | loop fusion | flops 21299200 | bytes 21299200 | tf_op jit(solution)/shard_map/concatenate | solution.py:57
  90.4 9.1 %reshape.87 = bf16[40,65,8,128]{3,2,1,0:T(8,128)(2,1)} reshape(bf16[40,65,1024]{2,1,0:T(8,128)(2,1)} %get-tuple-element.11) | data formatting | bytes 10649600 | tf_op jit(solution)/shard_map/reshape | solution.py:63
  99.5 9.3 %reshape.88 = bf16[40,65,8,128]{3,2,1,0:T(8,128)(2,1)} reshape(bf16[40,65,1024]{2,1,0:T(8,128)(2,1)} %get-tuple-element.12) | data formatting | bytes 10649600 | tf_op jit(solution)/shard_map/reshape | solution.py:64
  108.8 5.9 %fusion.4 = f32[40,8,1,65]{3,2,1,0:T(1,128)S(1)} fusion(bf16[40,65,8,128]{3,2,1,0:T(8,128)(2,1)} %reshape.87, bf16[40,3,1024]{2,1,0:T(4,128)(2,1)S(1)} %reshape.54), kind=kOutput, calls=%fused_computation.8 | convolution fusion | flops 5324800 | bytes 5571840 | tf_op jit(solution)/shard_map/thd,tjhd->thj/dot_general | solution.py:66
  114.6 0.2 fusion.10
  114.9 4.2 %fusion.2 = f32[40,8,1,128]{3,2,1,0:T(1,128)S(1)} fusion(bf16[40,65,8,128]{3,2,1,0:T(8,128)(2,1)} %reshape.88, bf16[40,8,65,1]{2,1,0,3:T(8,128)(2,1)S(1)} %fusion.10), kind=kOutput, calls=%fused_computation.6 | convolution fusion | flops 5324800 | bytes 5530240 | tf_op jit(solution)/shard_map/thj,tjhd->thd/dot_general | solution.py:70
  119.1 16.2 %all-gather.4.cloned.1.call-done = bf16[1024,4096]{1,0:T(8,128)(2,1)} async-done(((bf16[1024,512]{1,0:T(8,128)(2,1)}), bf16[1024,4096]{1,0:T(8,128)(2,1)}) %all-gather.4.cloned.1.call-update) | async-done | bytes 8388624 | tf_op jit(solution)/shard_map/all_gather | solution.py:76
  135.3 0.0 copy-start.2
  135.3 0.0 copy-start.1
  135.3 5.9 %fusion.19 = f32[40,4096]{1,0:T(8,128)} fusion(bf16[1024,4096]{1,0:T(8,128)(2,1)} %all-gather.4.cloned.1.call-done, bf16[5,8,8,128]{3,2,1,0:T(8,128)(2,1)S(1)} %bitcast.38), kind=kOutput, calls=%fused_computation.34 | convolution fusion | flops 335544320 | bytes 9125888 | tf_op jit(solution)/shard_map/dot_general | solution.py:74
  141.2 0.0 all-gather.6.cloned.1.call-update
  141.2 0.0 reduce-scatter.7.cloned.1.call-start
  141.3 0.0 copy-done.2
  141.3 0.1 copy.31
  141.4 0.7 dynamic-slice
  142.1 54.1 %all-gather.6.cloned.1.call-done = f32[160,4096]{1,0:T(8,128)} async-done(((f32[40,4096]{1,0:T(8,128)}), f32[160,4096]{1,0:T(8,128)}) %all-gather.6.cloned.1.call-update) | async-done | bytes 2621456 | tf_op jit(solution)/shard_map/all_gather | solution.py:79
  196.1 2.8 %reduce_sum.38 = f32[40,4096]{1,0:T(8,128)} reduce(f32[4,40,4096]{2,1,0:T(8,128)} %bitcast.35, f32[]{:T(128)} %constant.20.clone.1), dimensions={0}, to_apply=%region_4.6 | reduce | flops 491520 | bytes 3276804 | tf_op jit(solution)/shard_map/reduce_sum | solution.py:79
  198.9 0.0 copy-done.1
  198.9 1.3 multiply_reduce_fusion
  200.2 0.0 copy-done
  200.2 0.5 convolution_bitcast_fusion
  200.8 0.3 convolution_convert_fusion
  201.2 0.7 copy.44
  201.9 0.0 reduce-scatter.7.cloned.1.call-update
  201.9 0.8 convert_element_type.37
  202.7 17.5 %reduce-scatter.7.cloned.1.call-done = bf16[64,40]{1,0:T(8,128)(2,1)} async-done(((bf16[256,40]{1,0:T(8,128)(2,1)}), bf16[64,40]{1,0:T(8,128)(2,1)}) %reduce-scatter.7.cloned.1.call-update) | async-done | bytes 5136
  220.1 0.8 copy.43
  220.9 0.6 convert_element_type.41
  (6 shorter events, 0.1 us)
Async XLA Ops:
  7.2 193.1 %copy-start = (bf16[1024,1024]{1,0:T(8,128)(2,1)S(1)}, bf16[1024,1024]{1,0:T(8,128)(2,1)}, u32[]{:S(2)}) copy-start(bf16[1024,1024]{1,0:T(8,128)(2,1)} %param.17) | copy-start | bytes 6291460
  10.4 12.8 %all-to-all-start = ((bf16[40,8,512]{2,0,1:T(8,128)(2,1)}), bf16[40,8,512]{2,0,1:T(8,128)(2,1)S(1)}, u32[]{:S(2)}, u32[]{:S(2)}) async-start(bf16[40,8,512]{2,0,1:T(8,128)(2,1)} %bitcast.33), calls=%async_computation | async-start | bytes 655360 | tf_op jit(solution)/shard_map/all_to_all | solution.py:43
  15.6 62.0 %reduce-scatter.5.cloned.1.call-start = ((), (), s32[]{:S(2)}) async-start(), calls=%async_computation.3 | async-start | bytes 4423680 | tf_op jit(solution)/shard_map/reduce_scatter | solution.py:47
  23.2 5.8 %copy-start.3 = (s32[40]{0:T(128)S(1)}, s32[40]{0:T(128)}, u32[]{:S(2)}) copy-start(s32[40]{0:T(128)} %param.20) | copy-start | bytes 484
  28.2 107.1 %all-gather.4.cloned.1.call-start = ((), (), s32[]{:S(2)}) async-start(), calls=%async_computation.4 | async-start | bytes 9437184 | tf_op jit(solution)/shard_map/all_gather | solution.py:76
  29.0 167.2 %all-gather.6.cloned.1.call-start = ((), (), s32[]{:S(2)}) async-start(), calls=%async_computation.5 | async-start | bytes 3276800 | tf_op jit(solution)/shard_map/all_gather | solution.py:79
  135.3 6.0 %copy-start.2 = (s32[40,2]{0,1:T(2,128)S(1)}, s32[40,2]{0,1:T(2,128)}, u32[]{:S(2)}) copy-start(s32[40,2]{0,1:T(2,128)} %param.21) | copy-start | bytes 964
  135.3 63.6 %copy-start.1 = (bf16[40,4096]{1,0:T(8,128)(2,1)S(1)}, bf16[40,4096]{1,0:T(8,128)(2,1)}, u32[]{:S(2)}) copy-start(bf16[40,4096]{1,0:T(8,128)(2,1)} %param.12) | copy-start | bytes 983044
  141.2 78.9 %reduce-scatter.7.cloned.1.call-start = ((), (), s32[]{:S(2)}) async-start(), calls=%async_computation.6 | async-start | bytes 81920
Sparse Core Ops, SparseCore 0:
  28.3 49.1 reduce-scatter.4
  79.4 55.8 all-gather.3
  141.4 54.7 all-gather.5
  202.0 18.0 reduce-scatter.6
